TPU v7x, 32 devices: a whole 2x2x4 slice. The times are simulated.
32 devices in a mesh: row: 8 (over z, y), col: 4 (over x, core).
Axes of the slice: x: 2, y: 2, z: 4, core: 2. Of those that a mesh axis runs over, the one named last changes fastest.
Arguments:
- queries: bfloat16 [1024, 1024], P('row', 'col'), may hold values from -26 to 26
- key_vectors: bfloat16 [1024, 1024], P('row', 'col'), may hold values from -8 to 8
- values: bfloat16 [1024, 1024], P('row', 'col'), may hold values from -6 to 6
- sink_logit: float32 [8], P('col'), may hold values from -1 to 5
- lengths: int32 [8], replicated, may hold values from 1 to 576, as said below
- stream: bfloat16 [1024, 2048], P('row', 'col'), may hold values from -60 to 60
- out_weight: bfloat16 [1024, 2048], P('col', 'row'), may hold values from -0.1875 to 0.1875
- norm_gain: bfloat16 [2048], P('col'), may hold values from 0.25 to 1.75
- shared_gate: bfloat16 [2048, 2816], P('row', 'col'), may hold values from -0.125 to 0.125
- shared_up: bfloat16 [2048, 2816], P('row', 'col'), may hold values from -0.125 to 0.125
- shared_down: bfloat16 [2816, 2048], P('col', 'row'), may hold values from -0.109375 to 0.109375
- shared_switch: bfloat16 [2048], replicated, may hold values from -0.125 to 0.125
- expert_gate: bfloat16 [8, 2048, 1408], P('row', None, 'col'), may hold values from -0.125 to 0.125
- expert_up: bfloat16 [8, 2048, 1408], P('row', None, 'col'), may hold values from -0.125 to 0.125
- expert_down: bfloat16 [8, 1408, 2048], P('row', 'col'), may hold values from -0.15625 to 0.15625
- routes: int32 [1024, 4], P('row'), may hold values from 0 to 7, all different within a row; in each aligned block of 128 rows (0 to 127, 128 to 255, ...) at most 96 rows name the same one
- route_weights: float32 [1024, 4], P('row'), may hold values from 0.05 to 0.6
Outputs:
- attended: bfloat16 [1024, 1024], P('row', 'col')
- layer_out: bfloat16 [1024, 2048], P('row', 'col')
Inputs may be any that keep to these rules, and one draw needn't show every extreme that they name: `routes`: each row names 4 different experts; among the 128 rows of one device (aligned blocks) no expert is named more than 96 times, a bound that some block reaches. The lengths sum to 1024; exactly one prompt has 576 tokens.
All inputs are finite; a program needn't handle non-finite values.
Results may differ from a plain program's by a relative error of at most 0.01.
Values may be sent and summed in bfloat16 or wider, within the bound.
A program may use at most 128 MiB of HBM per device.

v0:
```python
import math
import jax
import jax.numpy as jnp
from jax import lax
from jax.sharding import PartitionSpec as P

HDIM = 128
WINDOW = 4096
norm_eps = 1e-06
masked_score = -1e30


def lower_bounds(lengths, positions):
    doc_ends = jnp.cumsum(lengths)
    starts = doc_ends - lengths
    begun_docs = starts[None, :] <= positions[:, None]
    doc_start = jnp.max(jnp.where(begun_docs, starts[None, :], 0), axis=1)
    return jnp.maximum(doc_start, positions - WINDOW + 1)


def body(
    queries,
    key_vectors,
    values,
    sink_logit,
    lengths,
    stream,
    out_weight,
    norm_gain,
    shared_gate,
    shared_up,
    shared_down,
    shared_switch,
    expert_gate,
    expert_up,
    expert_down,
    routes,
    route_weights,
):
    local_tokens = queries.shape[0]
    feature_width = queries.shape[1]
    head_count = feature_width // HDIM
    my_row = lax.axis_index("row")
    positions = my_row * local_tokens + jnp.arange(local_tokens, dtype=jnp.int32)
    lower_bound = lower_bounds(lengths, positions)
    query_heads = queries.reshape(local_tokens, head_count, HDIM)
    score_scale = 1.0 / math.sqrt(HDIM)
    key_value = jnp.stack([key_vectors, values], 0)
    key_piece = lax.all_gather(key_value, "row", axis=1, tiled=True)
    row_max = jnp.broadcast_to(sink_logit[None, :], (local_tokens, head_count))
    denominator = jnp.ones((local_tokens, head_count), jnp.float32)
    numerator = jnp.zeros((local_tokens, head_count, HDIM), jnp.float32)
    needed = key_piece.shape[1]
    key_heads = key_piece[0].reshape(needed, head_count, HDIM)
    value_heads = key_piece[1].reshape(needed, head_count, HDIM)
    scores = (
        jnp.einsum("qhd,khd->qhk", query_heads, key_heads, preferred_element_type=jnp.float32)
        * score_scale
    )
    key_places = jnp.arange(needed, dtype=jnp.int32)
    visible = (
        (key_places[None, :] >= lower_bound[:, None]) & (key_places[None, :] <= positions[:, None])
    )[:, None, :]
    masked = jnp.where(visible, scores, masked_score)
    new_max = jnp.maximum(row_max, jnp.max(masked, axis=2))
    weight = jnp.where(visible, jnp.exp(masked - new_max[:, :, None]), 0.0)
    rescale = jnp.exp(row_max - new_max)
    denominator = denominator * rescale + jnp.sum(weight, axis=2)
    numerator = numerator * rescale[:, :, None] + jnp.einsum(
        "qhk,khd->qhd", weight.astype(jnp.bfloat16), value_heads, preferred_element_type=jnp.float32
    )
    final_max, denominator, numerator = (new_max, denominator, numerator)
    attended = (
        (numerator / denominator[:, :, None])
        .reshape(local_tokens, feature_width)
        .astype(jnp.bfloat16)
    )
    head_terms = jnp.dot(
        attended,
        lax.all_gather(out_weight, "row", axis=1, tiled=True),
        preferred_element_type=jnp.float32,
    )
    mixed_heads = lax.psum_scatter(
        head_terms.astype(jnp.bfloat16), "col", scatter_dimension=1, tiled=True
    ).astype(jnp.float32)
    hidden = (stream.astype(jnp.float32) + mixed_heads).astype(jnp.bfloat16)
    widened = hidden.astype(jnp.float32)
    full_width = lax.axis_size("col") * hidden.shape[1]
    squares = lax.psum(jnp.sum(widened * widened, axis=1), "col")
    row_scale = lax.rsqrt(squares / full_width + norm_eps)
    normed_part = (widened * row_scale[:, None] * norm_gain.astype(jnp.float32)).astype(
        jnp.bfloat16
    )
    normed = lax.all_gather(normed_part, "col", axis=1, tiled=True)
    gate_part = jnp.dot(
        normed,
        lax.all_gather(shared_gate, "row", axis=0, tiled=True),
        preferred_element_type=jnp.float32,
    )
    up_part = jnp.dot(
        normed,
        lax.all_gather(shared_up, "row", axis=0, tiled=True),
        preferred_element_type=jnp.float32,
    )
    shared_act = (jax.nn.silu(gate_part) * up_part).astype(jnp.bfloat16)
    shared_part = jnp.dot(
        shared_act,
        lax.all_gather(shared_down, "row", axis=1, tiled=True),
        preferred_element_type=jnp.float32,
    )
    switch = jax.nn.sigmoid(jnp.dot(normed, shared_switch, preferred_element_type=jnp.float32))
    row_count = lax.axis_size("row")
    fanout = routes.shape[1]
    model_width = normed.shape[1]
    capacity = max(2, min(local_tokens, 3 * local_tokens * fanout // (2 * row_count)))
    flat_routes = routes.reshape(-1)
    onehot = (flat_routes[:, None] == jnp.arange(row_count, dtype=jnp.int32)[None, :]).astype(
        jnp.int32
    )
    before = jnp.cumsum(onehot, axis=0) - onehot
    slot_index = jnp.sum(before * onehot, axis=1)
    target = flat_routes * capacity + slot_index
    owner_row = jnp.arange(local_tokens * fanout, dtype=jnp.int32) // fanout
    source = jnp.full((row_count * capacity,), local_tokens, jnp.int32).at[target].set(owner_row)
    padded = jnp.concatenate([normed, jnp.zeros((1, model_width), jnp.bfloat16)], 0)
    outgoing = padded[source].reshape(row_count, capacity, model_width)
    received = lax.all_to_all(outgoing, "row", split_axis=0, concat_axis=0, tiled=True)
    senders, slot_count, received_width = received.shape
    dispatched = received.reshape(senders * slot_count, received_width)
    gate_out = jnp.dot(dispatched, expert_gate[0], preferred_element_type=jnp.float32)
    up_out = jnp.dot(dispatched, expert_up[0], preferred_element_type=jnp.float32)
    activation = (jax.nn.silu(gate_out) * up_out).astype(jnp.bfloat16)
    partial_out = jnp.dot(activation, expert_down[0], preferred_element_type=jnp.float32).astype(
        jnp.bfloat16
    )
    returned = lax.all_to_all(
        partial_out.reshape(senders, slot_count, received_width),
        "row",
        split_axis=0,
        concat_axis=0,
        tiled=True,
    )
    route_rows = returned.reshape(row_count * capacity, model_width)[target].reshape(
        local_tokens, fanout, model_width
    )
    routed = jnp.zeros((local_tokens, model_width), jnp.float32)
    for route_slot in range(fanout):
        routed = routed + route_weights[:, route_slot][:, None] * route_rows[
            :, route_slot, :
        ].astype(jnp.float32)
    layer_terms = switch[:, None] * shared_part + routed
    summed = lax.psum_scatter(
        layer_terms.astype(jnp.bfloat16), "col", scatter_dimension=1, tiled=True
    ).astype(jnp.float32)
    layer_out = (hidden.astype(jnp.float32) + summed).astype(jnp.bfloat16)
    return (attended, layer_out)


def solution(mesh):
    return jax.shard_map(
        body,
        mesh=mesh,
        in_specs=(
            P("row", "col"),
            P("row", "col"),
            P("row", "col"),
            P("col"),
            P(),
            P("row", "col"),
            P("col", "row"),
            P("col"),
            P("row", "col"),
            P("row", "col"),
            P("col", "row"),
            P(),
            P("row", None, "col"),
            P("row", None, "col"),
            P("row", "col", None),
            P("row", None),
            P("row", None),
        ),
        out_specs=(P("row", "col"), P("row", "col")),
        check_vma=False,
    )
```

profile of v0, /device:TPU:0, one launch (start us, length us, event | category | flops | bytes accessed | tf_op | source)
XLA Modules:
  0.0 430.8 jit_solution(6506192966484894538)
XLA Ops:
  7.2 1.1 copy.36
  8.3 1.0 copy.37
  9.3 0.7 pad_maximum_fusion
  10.0 0.7 all-gather.8.cloned.1.call-update
  10.8 0.8 reduce-window.19
  11.6 0.7 bitcast_subtract_fusion.1
  12.4 0.1 fusion.34
  12.5 40.4 %all-gather.6.cloned.1.call-done = bf16[2,1024,256]{1,2,0:T(8,128)(2,1)} async-done(((bf16[2,128,256]{1,2,0:T(8,128)(2,1)}), bf16[2,1024,256]{1,2,0:T(8,128)(2,1)}) %all-gather.6.cloned.1.call-update) | async-done | bytes 1048592 | tf_op jit(solution)/shard_map/all_gather | solution.py:49
  52.9 1.3 fusion.62
  54.2 0.4 fusion.63
  54.6 0.2 fusion.28
  55.0 0.4 fusion.18
  55.4 38.0 %all-gather.8.cloned.1.call-done = bf16[256,2048]{1,0:T(8,128)(2,1)} async-done(((bf16[256,256]{1,0:T(8,128)(2,1)}), bf16[256,2048]{1,0:T(8,128)(2,1)}) %all-gather.8.cloned.1.call-update) | async-done | bytes 1048592 | tf_op jit(solution)/shard_map/all_gather | solution.py:80
  93.4 2.4 convolution_convert_fusion.1
  95.9 0.5 all-gather.10.cloned.1.call-update
  96.4 0.1 copy.42
  96.6 0.1 eq.25
  96.8 1.1 reduce-window.20
  97.9 0.2 slice_reduce_fusion
  98.2 0.1 copy.41
  98.3 0.1 mul.135
  98.5 2.4 scatter_custom_fusion
  101.0 15.5 %reduce-scatter.3.cloned.1.call-done = bf16[128,512]{1,0:T(8,128)(2,1)} async-done(((bf16[128,2048]{1,0:T(8,128)(2,1)}), bf16[128,512]{1,0:T(8,128)(2,1)}) %reduce-scatter.3.cloned.1.call-update) | async-done | bytes 131088 | tf_op jit(solution)/shard_map/reduce_scatter | solution.py:83
  116.5 1.0 fusion.41
  117.5 5.8 %psum.7 = f32[128]{0:T(128)S(1)} all-reduce(f32[128]{0:T(128)S(1)} %fusion.41), channel_id=1, replica_groups=mesh['row'=8,'col'=4] {'col'}, use_global_device_ids=true, to_apply=%region_6.7 | all-reduce | flops 128 | bytes 1024 | tf_op jit(solution)/shard_map/psum | solution.py:89
  123.3 1.0 fusion.43
  124.3 7.3 %all_gather.20 = bf16[128,2048]{1,0:T(8,128)(2,1)S(1)} all-gather(bf16[128,512]{1,0:T(8,128)(2,1)S(1)} %fusion.43), channel_id=1, replica_groups=mesh['row'=8,'col'=4] {'col'}, dimensions={1}, use_global_device_ids=true | all-gather | bytes 655360 | tf_op jit(solution)/shard_map/all_gather | solution.py:94
  131.7 4.3 gather_fusion
  135.9 5.5 %all-to-all-start = ((bf16[8,96,2048]{2,1,0:T(8,128)(2,1)}), bf16[8,96,2048]{2,1,0:T(8,128)(2,1)}, u32[]{:S(2)}, u32[]{:S(2)}) async-start(bf16[8,96,2048]{2,1,0:T(8,128)(2,1)} %bitcast.109), calls=%async_computation.1 | async-start | bytes 6291456 | tf_op jit(solution)/shard_map/all_to_all | solution.py:127
  141.5 0.5 all-gather.12.cloned.1.call-update
  142.1 94.2 %all-to-all-done = bf16[8,96,2048]{2,1,0:T(8,128)(2,1)} async-done(((bf16[8,96,2048]{2,1,0:T(8,128)(2,1)}), bf16[8,96,2048]{2,1,0:T(8,128)(2,1)}, u32[]{:S(2)}, u32[]{:S(2)}) %all-to-all-start) | async-done | bytes 3145760 | tf_op jit(solution)/shard_map/all_to_all | solution.py:127
  236.2 4.7 %fusion.5 = f32[768,352]{0,1:T(8,128)} fusion(bf16[768,2048]{1,0:T(8,128)(2,1)} %bitcast.16, bf16[1,2048,352]{1,2,0:T(8,128)(2,1)} %param.29), kind=kOutput, calls=%fused_computation.11 | convolution fusion | flops 1107296256 | bytes 5668864 | tf_op jit(solution)/shard_map/dot_general | solution.py:130
  240.9 8.0 %convolution_convert_fusion = bf16[768,2048]{1,0:T(8,128)(2,1)} fusion(bf16[1,352,2048]{2,1,0:T(8,128)(2,1)S(1)} %copy-done, bf16[768,2048]{1,0:T(8,128)(2,1)} %bitcast.16, bf16[1,2048,352]{1,2,0:T(8,128)(2,1)} %param.30, f32[768,352]{0,1:T(8,128)} %fusion.5), kind=kOutput, calls=%fused_computation.3 | convolution fusion | flops 2217787392 | bytes 10256384 | tf_op jit(solution)/shard_map/dot_general | solution.py:133
  248.9 4.6 %all-to-all-start.1 = ((bf16[8,96,2048]{2,1,0:T(8,128)(2,1)}), bf16[8,96,2048]{2,1,0:T(8,128)(2,1)}, u32[]{:S(2)}, u32[]{:S(2)}) async-start(bf16[8,96,2048]{2,1,0:T(8,128)(2,1)} %bitcast.110), calls=%async_computation.2 | async-start | bytes 6291456 | tf_op jit(solution)/shard_map/all_to_all | solution.py:136
  253.6 0.5 all-gather.14.cloned.1.call-update
  254.1 0.2 reduce-scatter.5.cloned.1.call-start
  254.4 0.5 slice_bitcast_fusion.3
  254.9 0.3 fusion.22
  255.1 3.5 fusion.64
  258.6 92.9 %all-to-all-done.1 = bf16[8,96,2048]{2,1,0:T(8,128)(2,1)} async-done(((bf16[8,96,2048]{2,1,0:T(8,128)(2,1)}), bf16[8,96,2048]{2,1,0:T(8,128)(2,1)}, u32[]{:S(2)}, u32[]{:S(2)}) %all-to-all-start.1) | async-done | bytes 3145760 | tf_op jit(solution)/shard_map/all_to_all | solution.py:136
  351.5 7.5 %gather_fusion.1 = bf16[512,2048]{1,0:T(8,128)(2,1)} fusion(bf16[768,2048]{1,0:T(8,128)(2,1)} %bitcast.21, s32[1024]{0:T(1024)S(1)} %pad_clamp_fusion), kind=kCustom, calls=%fused_computation.1 | custom fusion | bytes 4196352 | tf_op jit(solution)/shard_map/gather | solution.py:143
  359.0 2.7 reshape.220
  361.8 4.5 %fusion.61 = (bf16[128,1,2048]{2,1,0:T(2,128)(2,1)}, bf16[128,1,2048]{2,1,0:T(2,128)(2,1)}, bf16[128,1,2048]{2,1,0:T(2,128)(2,1)}, bf16[128,1,2048]{2,1,0:T(2,128)(2,1)}) fusion(bf16[128,4,2048]{2,1,0:T(4,128)(2,1)S(1)} %reshape.220), kind=kLoop, calls=%fused_computation.104 | loop fusion | bytes 4194304 | tf_op jit(solution)/shard_map/slice | solution.py:148
  366.3 27.9 %all-gather.14.cloned.1.call-done = bf16[704,2048]{1,0:T(8,128)(2,1)} async-done(((bf16[704,256]{1,0:T(8,128)(2,1)}), bf16[704,2048]{1,0:T(8,128)(2,1)}) %all-gather.14.cloned.1.call-update) | async-done | bytes 2883600 | tf_op jit(solution)/shard_map/all_gather | solution.py:108
  394.2 8.1 %fusion.1 = bf16[128,2048]{1,0:T(8,128)(2,1)} fusion(bf16[704,2048]{1,0:T(8,128)(2,1)} %all-gather.14.cloned.1.call-done, bf16[128,2048]{1,0:T(8,128)(2,1)} %copy-done.1, bf16[2048,704]{0,1:T(8,128)(2,1)} %all-gather.12.cloned.1.call-done, bf16[128,1,2048]{2,1,0:T(2,128)(2,1)} %get-tuple-element.11, bf16[128,1,2048]{2,1,0:T(2,128)(2,1)} %get-tuple-element.9, ...), kind=kOutput, calls=%fused_computation.6 | convolution fusion | flops 742408192 | bytes 9275904 | tf_op jit(solution)/shard_map/dot_general | solution.py:106
  402.3 0.7 copy.48
  403.1 19.3 %reduce-scatter.5.cloned.1.call-done = bf16[128,512]{1,0:T(8,128)(2,1)} async-done(((bf16[128,2048]{1,0:T(8,128)(2,1)}), bf16[128,512]{1,0:T(8,128)(2,1)}) %reduce-scatter.5.cloned.1.call-update) | async-done | bytes 131088 | tf_op jit(solution)/shard_map/reduce_scatter | solution.py:152
  422.3 1.6 fusion.44
  (57 shorter events, 0.9 us)
Async XLA Ops:
  7.2 233.7 %copy-start = (bf16[1,352,2048]{2,1,0:T(8,128)(2,1)S(1)}, bf16[1,352,2048]{2,1,0:T(8,128)(2,1)}, u32[]{:S(2)}) copy-start(bf16[1,352,2048]{2,1,0:T(8,128)(2,1)} %param.31) | copy-start | bytes 4325380
  7.2 47.0 %copy-start.7 = (bf16[128,256]{1,0:T(8,128)(2,1)S(1)}, bf16[128,256]{1,0:T(8,128)(2,1)}, u32[]{:S(2)}) copy-start(bf16[128,256]{1,0:T(8,128)(2,1)} %param.17) | copy-start | bytes 196612
  7.2 45.7 %all-gather.6.cloned.1.call-start = ((), (), s32[]{:S(2)}) async-start(), calls=%async_computation.4 | async-start | bytes 1179648 | tf_op jit(solution)/shard_map/all_gather | solution.py:49
  10.0 44.6 %copy-start.10 = (f32[2]{0:T(128)S(1)}, f32[2]{0:T(128)}, u32[]{:S(2)}) copy-start(f32[2]{0:T(128)} %param.20) | copy-start | bytes 28
  10.0 83.4 %all-gather.8.cloned.1.call-start = ((), (), s32[]{:S(2)}) async-start(), calls=%async_computation.5 | async-start | bytes 1179648 | tf_op jit(solution)/shard_map/all_gather | solution.py:80
  10.7 105.8 %reduce-scatter.3.cloned.1.call-start = ((), (), s32[]{:S(2)}) async-start(), calls=%async_computation.6 | async-start | bytes 655360 | tf_op jit(solution)/shard_map/reduce_scatter | solution.py:83
  54.9 41.4 %copy-start.8 = (s32[128,4]{0,1:T(4,128)S(1)}, s32[128,4]{0,1:T(4,128)}, u32[]{:S(2)}) copy-start(s32[128,4]{0,1:T(4,128)} %param.32) | copy-start | bytes 6148
  54.9 41.8 %copy-start.12 = (bf16[512]{0:T(512)(128)(2,1)S(1)}, bf16[512]{0:T(512)(128)(2,1)}, u32[]{:S(2)}) copy-start(bf16[512]{0:T(512)(128)(2,1)} %param.24) | copy-start | bytes 3076
  55.3 40.5 %copy-start.5 = (bf16[128,2,128]{0,2,1:T(8,128)(2,1)}, bf16[128,2,128]{0,2,1:T(8,128)(2,1)S(1)}, u32[]{:S(2)}) copy-start(bf16[128,2,128]{0,2,1:T(8,128)(2,1)S(1)} %fusion.18) | copy-start | bytes 196612
  55.4 61.1 %copy-start.2 = (bf16[128,512]{1,0:T(8,128)(2,1)S(1)}, bf16[128,512]{1,0:T(8,128)(2,1)}, u32[]{:S(2)}) copy-start(bf16[128,512]{1,0:T(8,128)(2,1)} %param.22) | copy-start | bytes 393220
  95.8 159.3 %all-gather.10.cloned.1.call-start = ((), (), s32[]{:S(2)}) async-start(), calls=%async_computation.7 | async-start | bytes 3244032 | tf_op jit(solution)/shard_map/all_gather | solution.py:97
  131.6 123.5 %copy-start.1 = (bf16[128,2048]{1,0:T(8,128)(2,1)}, bf16[128,2048]{1,0:T(8,128)(2,1)S(1)}, u32[]{:S(2)}) copy-start(bf16[128,2048]{1,0:T(8,128)(2,1)S(1)} %all_gather.20) | copy-start | bytes 1572868
  135.9 100.3 %all-to-all-start = ((bf16[8,96,2048]{2,1,0:T(8,128)(2,1)}), bf16[8,96,2048]{2,1,0:T(8,128)(2,1)}, u32[]{:S(2)}, u32[]{:S(2)}) async-start(bf16[8,96,2048]{2,1,0:T(8,128)(2,1)} %bitcast.109), calls=%async_computation.1 | async-start | bytes 6291456 | tf_op jit(solution)/shard_map/all_to_all | solution.py:127
  141.5 224.8 %all-gather.12.cloned.1.call-start = ((), (), s32[]{:S(2)}) async-start(), calls=%async_computation.8 | async-start | bytes 3244032 | tf_op jit(solution)/shard_map/all_gather | solution.py:102
  248.9 5.4 %copy-start.9 = (bf16[2048]{0:T(1024)(128)(2,1)S(1)}, bf16[2048]{0:T(1024)(128)(2,1)}, u32[]{:S(2)}) copy-start(bf16[2048]{0:T(1024)(128)(2,1)} %param.28) | copy-start | bytes 12292
  248.9 5.4 %copy-start.11 = (f32[128,4]{0,1:T(4,128)S(1)}, f32[128,4]{0,1:T(4,128)}, u32[]{:S(2)}) copy-start(f32[128,4]{0,1:T(4,128)} %param.33) | copy-start | bytes 6148
  248.9 102.6 %all-to-all-start.1 = ((bf16[8,96,2048]{2,1,0:T(8,128)(2,1)}), bf16[8,96,2048]{2,1,0:T(8,128)(2,1)}, u32[]{:S(2)}, u32[]{:S(2)}) async-start(bf16[8,96,2048]{2,1,0:T(8,128)(2,1)} %bitcast.110), calls=%async_computation.2 | async-start | bytes 6291456 | tf_op jit(solution)/shard_map/all_to_all | solution.py:136
  253.5 140.7 %all-gather.14.cloned.1.call-start = ((), (), s32[]{:S(2)}) async-start(), calls=%async_computation.9 | async-start | bytes 3244032 | tf_op jit(solution)/shard_map/all_gather | solution.py:108
  254.1 168.3 %reduce-scatter.5.cloned.1.call-start = ((), (), s32[]{:S(2)}) async-start(), calls=%async_computation.10 | async-start | bytes 655360 | tf_op jit(solution)/shard_map/reduce_scatter | solution.py:152
  394.2 8.1 %copy-start.6 = (bf16[128,2,128]{0,2,1:T(8,128)(2,1)S(1)}, bf16[128,2,128]{0,2,1:T(8,128)(2,1)}, u32[]{:S(2)}) copy-start(bf16[128,2,128]{0,2,1:T(8,128)(2,1)} %copy-done.5) | copy-start | bytes 196612
  394.2 28.1 %copy-start.3 = (bf16[128,512]{1,0:T(8,128)(2,1)S(1)}, bf16[128,512]{1,0:T(8,128)(2,1)}, u32[]{:S(2)}) copy-start(bf16[128,512]{1,0:T(8,128)(2,1)} %param.22) | copy-start | bytes 393220
  394.2 28.1 %copy-start.4 = (bf16[128,512]{1,0:T(8,128)(2,1)S(1)}, bf16[128,512]{1,0:T(8,128)(2,1)}, u32[]{:S(2)}) copy-start(bf16[128,512]{1,0:T(8,128)(2,1)} %reduce-scatter.3.cloned.1.call-done) | copy-start | bytes 393220
Sparse Core Ops, SparseCore 0:
  10.6 42.2 all-gather.5
  55.0 38.4 all-gather.7
  95.9 20.5 reduce-scatter.2
  118.6 109.6 all-gather.9
  230.3 102.7 all-gather.11
  335.3 58.9 all-gather.13
  402.4 19.8 reduce-scatter.4
where the time goes:
time: 431 us
  waiting for transfers between devices  330 us (77%)
  matrix products  27.7 us (6%)
  local copies, waits for them, and re-layouts  26.9 us (6%)
  between operations  14.4 us (3%)
  blocking collectives  13.1 us (3%)
  starting transfers between devices  10.6 us (2%)
  other arithmetic  7.72 us (2%)
    all_to_all x1, waiting for transfers between devices, body(): lax.all_to_all(outgoing, 'row', split_axis=0, concat_axis=0, tiled=True)  94.2 us
    all_to_all x1, waiting for transfers between devices, body(): lax.all_to_all(partial_out.reshape(senders, slot_count, received_width),...  92.9 us
    all_gather x1, waiting for transfers between devices, body(): key_piece = lax.all_gather(key_value, 'row', axis=1, tiled=True)  40.4 us
    all_gather x1, waiting for transfers between devices, body(): lax.all_gather(out_weight, 'row', axis=1, tiled=True)  38 us
    all_gather x1, waiting for transfers between devices, body(): lax.all_gather(shared_down, 'row', axis=1, tiled=True)  27.9 us
    reduce_scatter x1, waiting for transfers between devices, body(): lax.psum_scatter(layer_terms.astype(jnp.bfloat16), 'col', scatter_dimensi...  19.3 us
    reduce_scatter x1, waiting for transfers between devices, body(): lax.psum_scatter(head_terms.astype(jnp.bfloat16), 'col', scatter_dimensio...  15.5 us
  transfers between devices with their start and end apart: 9, of which 7 were waited for; matrix products, arithmetic and copies ran while one was open for 11% of the time, Pallas kernels for 0%

commit v1 on v0

--- a/solution.py
+++ b/solution.py
@@ -46,7 +46,14 @@
     query_heads = queries.reshape(local_tokens, head_count, HDIM)
     score_scale = 1.0 / math.sqrt(HDIM)
     key_value = jnp.stack([key_vectors, values], 0)
-    key_piece = lax.all_gather(key_value, "row", axis=1, tiled=True)
+    ways, here, step = (lax.axis_size("row"), lax.axis_index("row"), key_value.shape[1])
+    line, have = (key_value, 1)
+    while have < ways:
+        line = jnp.concatenate(
+            [line, lax.ppermute(line, "row", [(d, (d - have) % ways) for d in range(ways)])], axis=1
+        )
+        have = 2 * have
+    key_piece = jnp.roll(line, here * step, axis=1)
     row_max = jnp.broadcast_to(sink_logit[None, :], (local_tokens, head_count))
     denominator = jnp.ones((local_tokens, head_count), jnp.float32)
     numerator = jnp.zeros((local_tokens, head_count, HDIM), jnp.float32)

time: 431 us -> 407 us (0.944)
  waiting for transfers between devices: 330 us -> 293 us
  starting transfers between devices: 10.6 us -> 18.1 us
  local copies, waits for them, and re-layouts: 26.9 us -> 31.6 us
    all_gather x1 -> x0, waiting for transfers between devices: 40.4 us -> none  [body(): key_piece = lax.all_gather(key_value, 'row', axis=1, tiled=True)]
    ppermute x0 -> x3, waiting for transfers between devices: none -> 32.1 us  [body(): lax.ppermute(line, 'row', [(d, (d - have) % ways) for d in range(ways)])]
    all_gather x1, waiting for transfers between devices: 38 us -> 6.65 us  [body(): lax.all_gather(out_weight, 'row', axis=1, tiled=True)]
    all_gather x1, waiting for transfers between devices: 27.9 us -> 0.01 us  [body(): lax.all_gather(shared_down, 'row', axis=1, tiled=True)]
    all_gather x1, waiting for transfers between devices: 0.01 us -> 27.7 us  [body(): lax.all_gather(shared_up, 'row', axis=0, tiled=True)]
    ppermute x0 -> x3, starting transfers between devices: none -> 7.65 us  [body(): lax.ppermute(line, 'row', [(d, (d - have) % ways) for d in range(ways)])]
  transfers between devices with their start and end apart: 9 -> 11, of which waited for: 7 -> 9; matrix products, arithmetic and copies ran while one was open for 11% -> 13% of each run, Pallas kernels for 0% -> 0%
where the time goes in v1:
time: 407 us
  waiting for transfers between devices  293 us (72%)
  local copies, waits for them, and re-layouts  31.6 us (8%)
  matrix products  27.7 us (7%)
  starting transfers between devices  18.1 us (4%)
  between operations  14.4 us (4%)
  blocking collectives  13.1 us (3%)
  other arithmetic  8.49 us (2%)
    all_to_all x1, waiting for transfers between devices, body(): lax.all_to_all(outgoing, 'row', split_axis=0, concat_axis=0, tiled=True)  94.3 us
    all_to_all x1, waiting for transfers between devices, body(): lax.all_to_all(partial_out.reshape(senders, slot_count, received_width),...  93.1 us
    ppermute x3, waiting for transfers between devices, body(): lax.ppermute(line, 'row', [(d, (d - have) % ways) for d in range(ways)])  32.1 us
    all_gather x1, waiting for transfers between devices, body(): lax.all_gather(shared_up, 'row', axis=0, tiled=True)  27.7 us
    reduce_scatter x1, waiting for transfers between devices, body(): lax.psum_scatter(layer_terms.astype(jnp.bfloat16), 'col', scatter_dimensi...  19.2 us
    reduce_scatter x1, waiting for transfers between devices, body(): lax.psum_scatter(head_terms.astype(jnp.bfloat16), 'col', scatter_dimensio...  18.6 us
  transfers between devices with their start and end apart: 11, of which 9 were waited for; matrix products, arithmetic and copies ran while one was open for 13% of the time, Pallas kernels for 0%

profile of v1, /device:TPU:0, one launch (start us, length us, event | category | flops | bytes accessed | tf_op | source)
XLA Modules:
  0.0 406.8 jit_solution(2784416721896887481)
XLA Ops:
  7.2 1.1 copy.36
  8.3 1.0 copy.37
  9.2 0.7 pad_maximum_fusion.2
  9.9 6.0 %collective-permute-start = (bf16[2,128,256]{1,2,0:T(8,128)(2,1)S(1)}, bf16[2,128,256]{1,2,0:T(8,128)(2,1)S(1)}, u32[]{:S(2)}, u32[]{:S(2)}) collective-permute-start(bf16[2,128,256]{1,2,0:T(8,128)(2,1)S(1)} %get-tuple-element.14), channel_id=1, source_target_pairs={{0,28},{4,0},{8,4},{12,8},{16,12},{20,16},{24,20},{28,24},{1,29},{... | collective-permute-start | bytes 393224 | tf_op jit(solution)/shard_map/ppermute | solution.py:53
  16.0 0.8 reduce-window.19
  16.8 1.8 collective-permute-done
  18.7 1.6 collective-permute-start.1
  20.3 0.7 bitcast_subtract_fusion.1
  21.1 8.1 %collective-permute-done.1 = bf16[2,256,256]{1,2,0:T(8,128)(2,1)S(1)} collective-permute-done((bf16[2,256,256]{1,2,0:T(8,128)(2,1)S(1)}, bf16[2,256,256]{1,2,0:T(8,128)(2,1)S(1)}, u32[]{:S(2)}, u32[]{:S(2)}) %collective-permute-start.1) | collective-permute-done | bytes 262176 | tf_op jit(solution)/shard_map/ppermute | solution.py:53
  29.4 0.7 constant_dynamic-update-slice_fusion.6
  30.1 0.7 constant_dynamic-update-slice_fusion.5
  30.9 22.1 %collective-permute-done.2 = bf16[2,512,256]{1,2,0:T(8,128)(2,1)S(1)} collective-permute-done((bf16[2,512,256]{1,2,0:T(8,128)(2,1)S(1)}, bf16[2,512,256]{1,2,0:T(8,128)(2,1)S(1)}, u32[]{:S(2)}, u32[]{:S(2)}) %collective-permute-start.2) | collective-permute-done | bytes 524320 | tf_op jit(solution)/shard_map/ppermute | solution.py:53
  53.0 0.9 constant_dynamic-update-slice_fusion.4
  53.9 0.7 constant_dynamic-update-slice_fusion.3
  54.6 0.7 constant_dynamic-update-slice_fusion.2
  55.3 0.7 constant_dynamic-update-slice_fusion.1
  56.0 0.9 constant_dynamic-update-slice_fusion
  56.9 1.3 constant_dynamic-slice_fusion
  59.0 0.4 fusion.18
  59.4 6.7 %all-gather.5.cloned.1.call-done = bf16[256,2048]{1,0:T(8,128)(2,1)} async-done(((bf16[256,256]{1,0:T(8,128)(2,1)}), bf16[256,2048]{1,0:T(8,128)(2,1)}) %all-gather.5.cloned.1.call-update) | async-done | bytes 1048592 | tf_op jit(solution)/shard_map/all_gather | solution.py:87
  66.0 2.4 convolution_convert_fusion.1
  68.5 0.7 all-gather.7.cloned.1.call-update
  69.5 1.1 reduce-window.20
  71.3 2.4 scatter_custom_fusion
  73.8 18.6 %reduce-scatter.3.cloned.1.call-done = bf16[128,512]{1,0:T(8,128)(2,1)} async-done(((bf16[128,2048]{1,0:T(8,128)(2,1)}), bf16[128,512]{1,0:T(8,128)(2,1)}) %reduce-scatter.3.cloned.1.call-update) | async-done | bytes 131088 | tf_op jit(solution)/shard_map/reduce_scatter | solution.py:90
  92.4 1.0 fusion.41
  93.4 5.8 %psum.7 = f32[128]{0:T(128)S(1)} all-reduce(f32[128]{0:T(128)S(1)} %fusion.41), channel_id=1, replica_groups=mesh['row'=8,'col'=4] {'col'}, use_global_device_ids=true, to_apply=%region_6.7 | all-reduce | flops 128 | bytes 1024 | tf_op jit(solution)/shard_map/psum | solution.py:96
  99.2 1.0 fusion.43
  100.2 7.3 %all_gather.16 = bf16[128,2048]{1,0:T(8,128)(2,1)S(1)} all-gather(bf16[128,512]{1,0:T(8,128)(2,1)S(1)} %fusion.43), channel_id=1, replica_groups=mesh['row'=8,'col'=4] {'col'}, dimensions={1}, use_global_device_ids=true | all-gather | bytes 655360 | tf_op jit(solution)/shard_map/all_gather | solution.py:101
  107.6 4.3 %gather_fusion = bf16[768,2048]{1,0:T(8,128)(2,1)} fusion(bf16[129,2048]{1,0:T(8,128)(2,1)S(1)} %concatenate.20, s32[1024]{0:T(1024)S(1)} %pad_clamp_fusion.1), kind=kCustom, calls=%fused_computation | custom fusion | bytes 6294528 | tf_op jit(solution)/shard_map/gather | solution.py:133
  111.8 5.5 %all-to-all-start = ((bf16[8,96,2048]{2,1,0:T(8,128)(2,1)}), bf16[8,96,2048]{2,1,0:T(8,128)(2,1)}, u32[]{:S(2)}, u32[]{:S(2)}) async-start(bf16[8,96,2048]{2,1,0:T(8,128)(2,1)} %bitcast.109), calls=%async_computation.1 | async-start | bytes 6291456 | tf_op jit(solution)/shard_map/all_to_all | solution.py:134
  117.4 0.5 all-gather.11.cloned.1.call-update
  117.9 94.3 %all-to-all-done = bf16[8,96,2048]{2,1,0:T(8,128)(2,1)} async-done(((bf16[8,96,2048]{2,1,0:T(8,128)(2,1)}), bf16[8,96,2048]{2,1,0:T(8,128)(2,1)}, u32[]{:S(2)}, u32[]{:S(2)}) %all-to-all-start) | async-done | bytes 3145760 | tf_op jit(solution)/shard_map/all_to_all | solution.py:134
  212.2 4.7 %fusion.5 = f32[768,352]{0,1:T(8,128)} fusion(bf16[768,2048]{1,0:T(8,128)(2,1)} %bitcast.16, bf16[1,2048,352]{1,2,0:T(8,128)(2,1)} %param.29), kind=kOutput, calls=%fused_computation.11 | convolution fusion | flops 1107296256 | bytes 5668864 | tf_op jit(solution)/shard_map/dot_general | solution.py:137
  216.9 8.0 %convolution_convert_fusion = bf16[768,2048]{1,0:T(8,128)(2,1)} fusion(bf16[1,352,2048]{2,1,0:T(8,128)(2,1)S(1)} %copy-done, bf16[768,2048]{1,0:T(8,128)(2,1)} %bitcast.16, bf16[1,2048,352]{1,2,0:T(8,128)(2,1)} %param.30, f32[768,352]{0,1:T(8,128)} %fusion.5), kind=kOutput, calls=%fused_computation.3 | convolution fusion | flops 2217787392 | bytes 10256384 | tf_op jit(solution)/shard_map/dot_general | solution.py:140
  224.9 4.6 %all-to-all-start.1 = ((bf16[8,96,2048]{2,1,0:T(8,128)(2,1)}), bf16[8,96,2048]{2,1,0:T(8,128)(2,1)}, u32[]{:S(2)}, u32[]{:S(2)}) async-start(bf16[8,96,2048]{2,1,0:T(8,128)(2,1)} %bitcast.110), calls=%async_computation.2 | async-start | bytes 6291456 | tf_op jit(solution)/shard_map/all_to_all | solution.py:143
  229.6 0.5 all-gather.9.cloned.1.call-update
  230.4 0.5 slice_bitcast_fusion.3
  231.2 3.5 fusion.63
  234.7 93.1 %all-to-all-done.1 = bf16[8,96,2048]{2,1,0:T(8,128)(2,1)} async-done(((bf16[8,96,2048]{2,1,0:T(8,128)(2,1)}), bf16[8,96,2048]{2,1,0:T(8,128)(2,1)}, u32[]{:S(2)}, u32[]{:S(2)}) %all-to-all-start.1) | async-done | bytes 3145760 | tf_op jit(solution)/shard_map/all_to_all | solution.py:143
  327.7 7.5 %gather_fusion.1 = bf16[512,2048]{1,0:T(8,128)(2,1)} fusion(bf16[768,2048]{1,0:T(8,128)(2,1)} %bitcast.21, s32[1024]{0:T(1024)S(1)} %pad_clamp_fusion), kind=kCustom, calls=%fused_computation.1 | custom fusion | bytes 4196352 | tf_op jit(solution)/shard_map/gather | solution.py:150
  335.3 2.7 reshape.220
  338.0 4.5 %fusion.61 = (bf16[128,1,2048]{2,1,0:T(2,128)(2,1)}, bf16[128,1,2048]{2,1,0:T(2,128)(2,1)}, bf16[128,1,2048]{2,1,0:T(2,128)(2,1)}, bf16[128,1,2048]{2,1,0:T(2,128)(2,1)}) fusion(bf16[128,4,2048]{2,1,0:T(4,128)(2,1)S(1)} %reshape.220), kind=kLoop, calls=%fused_computation.116 | loop fusion | bytes 4194304 | tf_op jit(solution)/shard_map/slice | solution.py:155
  342.5 27.7 %all-gather.9.cloned.1.call-done = bf16[2048,704]{0,1:T(8,128)(2,1)} async-done(((bf16[256,704]{0,1:T(8,128)(2,1)}), bf16[2048,704]{0,1:T(8,128)(2,1)}) %all-gather.9.cloned.1.call-update) | async-done | bytes 2883600 | tf_op jit(solution)/shard_map/all_gather | solution.py:109
  370.2 8.1 %fusion.1 = bf16[128,2048]{1,0:T(8,128)(2,1)} fusion(bf16[704,2048]{1,0:T(8,128)(2,1)} %all-gather.11.cloned.1.call-done, bf16[128,2048]{1,0:T(8,128)(2,1)} %copy-done.1, bf16[2048,704]{0,1:T(8,128)(2,1)} %all-gather.9.cloned.1.call-done, bf16[128,1,2048]{2,1,0:T(2,128)(2,1)} %get-tuple-element.11, bf16[128,1,2048]{2,1,0:T(2,128)(2,1)} %get-tuple-element.9, ...), kind=kOutput, calls=%fused_computation.6 | convolution fusion | flops 742408192 | bytes 9275904 | tf_op jit(solution)/shard_map/dot_general | solution.py:113
  378.3 0.7 copy.48
  379.1 19.2 %reduce-scatter.5.cloned.1.call-done = bf16[128,512]{1,0:T(8,128)(2,1)} async-done(((bf16[128,2048]{1,0:T(8,128)(2,1)}), bf16[128,512]{1,0:T(8,128)(2,1)}) %reduce-scatter.5.cloned.1.call-update) | async-done | bytes 131088 | tf_op jit(solution)/shard_map/reduce_scatter | solution.py:159
  398.3 1.6 fusion.44
  (69 shorter events, 2.9 us)
Async XLA Ops:
  7.2 209.8 %copy-start = (bf16[1,352,2048]{2,1,0:T(8,128)(2,1)S(1)}, bf16[1,352,2048]{2,1,0:T(8,128)(2,1)}, u32[]{:S(2)}) copy-start(bf16[1,352,2048]{2,1,0:T(8,128)(2,1)} %param.31) | copy-start | bytes 4325380
  7.2 58.9 %all-gather.5.cloned.1.call-start = ((), (), s32[]{:S(2)}) async-start(), calls=%async_computation.4 | async-start | bytes 1179648 | tf_op jit(solution)/shard_map/all_gather | solution.py:87
  9.9 8.8 %collective-permute-start = (bf16[2,128,256]{1,2,0:T(8,128)(2,1)S(1)}, bf16[2,128,256]{1,2,0:T(8,128)(2,1)S(1)}, u32[]{:S(2)}, u32[]{:S(2)}) collective-permute-start(bf16[2,128,256]{1,2,0:T(8,128)(2,1)S(1)} %get-tuple-element.14), channel_id=1, source_target_pairs={{0,28},{4,0},{8,4},{12,8},{16,12},{20,16},{24,20},{28,24},{1,29},{... | collective-permute-start | bytes 393224 | tf_op jit(solution)/shard_map/ppermute | solution.py:53
  16.0 76.4 %reduce-scatter.3.cloned.1.call-start = ((), (), s32[]{:S(2)}) async-start(), calls=%async_computation.5 | async-start | bytes 655360 | tf_op jit(solution)/shard_map/reduce_scatter | solution.py:90
  18.7 10.4 %collective-permute-start.1 = (bf16[2,256,256]{1,2,0:T(8,128)(2,1)S(1)}, bf16[2,256,256]{1,2,0:T(8,128)(2,1)S(1)}, u32[]{:S(2)}, u32[]{:S(2)}) collective-permute-start(bf16[2,256,256]{1,2,0:T(8,128)(2,1)S(1)} %pad_maximum_fusion.1), channel_id=1, source_target_pairs={{0,24},{4,28},{8,0},{12,4},{16,8},{20,12},{24,16},{28,20},{1,25},{... | collective-permute-start | bytes 786440 | tf_op jit(solution)/shard_map/ppermute | solution.py:53
  29.2 23.8 %collective-permute-start.2 = (bf16[2,512,256]{1,2,0:T(8,128)(2,1)S(1)}, bf16[2,512,256]{1,2,0:T(8,128)(2,1)S(1)}, u32[]{:S(2)}, u32[]{:S(2)}) collective-permute-start(bf16[2,512,256]{1,2,0:T(8,128)(2,1)S(1)} %pad_maximum_fusion), channel_id=1, source_target_pairs={{0,16},{4,20},{8,24},{12,28},{16,0},{20,4},{24,8},{28,12},{1,17},{... | collective-permute-start | bytes 1572872 | tf_op jit(solution)/shard_map/ppermute | solution.py:53
  53.9 4.3 %copy-start.7 = (bf16[128,256]{1,0:T(8,128)(2,1)S(1)}, bf16[128,256]{1,0:T(8,128)(2,1)}, u32[]{:S(2)}) copy-start(bf16[128,256]{1,0:T(8,128)(2,1)} %param.17) | copy-start | bytes 196612
  56.9 1.7 copy-start.10
  59.0 10.2 %copy-start.8 = (s32[128,4]{0,1:T(4,128)S(1)}, s32[128,4]{0,1:T(4,128)}, u32[]{:S(2)}) copy-start(s32[128,4]{0,1:T(4,128)} %param.32) | copy-start | bytes 6148
  59.0 10.5 %copy-start.12 = (bf16[512]{0:T(512)(128)(2,1)S(1)}, bf16[512]{0:T(512)(128)(2,1)}, u32[]{:S(2)}) copy-start(bf16[512]{0:T(512)(128)(2,1)} %param.24) | copy-start | bytes 3076
  59.4 9.1 %copy-start.5 = (bf16[128,2,128]{0,2,1:T(8,128)(2,1)}, bf16[128,2,128]{0,2,1:T(8,128)(2,1)S(1)}, u32[]{:S(2)}) copy-start(bf16[128,2,128]{0,2,1:T(8,128)(2,1)S(1)} %fusion.18) | copy-start | bytes 196612
  59.4 33.0 %copy-start.2 = (bf16[128,512]{1,0:T(8,128)(2,1)S(1)}, bf16[128,512]{1,0:T(8,128)(2,1)}, u32[]{:S(2)}) copy-start(bf16[128,512]{1,0:T(8,128)(2,1)} %param.22) | copy-start | bytes 393220
  68.4 162.8 %all-gather.7.cloned.1.call-start = ((), (), s32[]{:S(2)}) async-start(), calls=%async_computation.6 | async-start | bytes 3244032 | tf_op jit(solution)/shard_map/all_gather | solution.py:104
  107.5 123.7 %copy-start.1 = (bf16[128,2048]{1,0:T(8,128)(2,1)}, bf16[128,2048]{1,0:T(8,128)(2,1)S(1)}, u32[]{:S(2)}) copy-start(bf16[128,2048]{1,0:T(8,128)(2,1)S(1)} %all_gather.16) | copy-start | bytes 1572868
  111.8 100.4 %all-to-all-start = ((bf16[8,96,2048]{2,1,0:T(8,128)(2,1)}), bf16[8,96,2048]{2,1,0:T(8,128)(2,1)}, u32[]{:S(2)}, u32[]{:S(2)}) async-start(bf16[8,96,2048]{2,1,0:T(8,128)(2,1)} %bitcast.109), calls=%async_computation.1 | async-start | bytes 6291456 | tf_op jit(solution)/shard_map/all_to_all | solution.py:134
  117.3 225.2 %all-gather.11.cloned.1.call-start = ((), (), s32[]{:S(2)}) async-start(), calls=%async_computation.8 | async-start | bytes 3244032 | tf_op jit(solution)/shard_map/all_gather | solution.py:115
  224.9 5.4 %copy-start.9 = (bf16[2048]{0:T(1024)(128)(2,1)S(1)}, bf16[2048]{0:T(1024)(128)(2,1)}, u32[]{:S(2)}) copy-start(bf16[2048]{0:T(1024)(128)(2,1)} %param.28) | copy-start | bytes 12292
  224.9 5.4 %copy-start.11 = (f32[128,4]{0,1:T(4,128)S(1)}, f32[128,4]{0,1:T(4,128)}, u32[]{:S(2)}) copy-start(f32[128,4]{0,1:T(4,128)} %param.33) | copy-start | bytes 6148
  224.9 102.8 %all-to-all-start.1 = ((bf16[8,96,2048]{2,1,0:T(8,128)(2,1)}), bf16[8,96,2048]{2,1,0:T(8,128)(2,1)}, u32[]{:S(2)}, u32[]{:S(2)}) async-start(bf16[8,96,2048]{2,1,0:T(8,128)(2,1)} %bitcast.110), calls=%async_computation.2 | async-start | bytes 6291456 | tf_op jit(solution)/shard_map/all_to_all | solution.py:143
  229.5 140.7 %all-gather.9.cloned.1.call-start = ((), (), s32[]{:S(2)}) async-start(), calls=%async_computation.7 | async-start | bytes 3244032 | tf_op jit(solution)/shard_map/all_gather | solution.py:109
  230.1 168.2 %reduce-scatter.5.cloned.1.call-start = ((), (), s32[]{:S(2)}) async-start(), calls=%async_computation.9 | async-start | bytes 655360 | tf_op jit(solution)/shard_map/reduce_scatter | solution.py:159
  370.2 8.1 %copy-start.6 = (bf16[128,2,128]{0,2,1:T(8,128)(2,1)S(1)}, bf16[128,2,128]{0,2,1:T(8,128)(2,1)}, u32[]{:S(2)}) copy-start(bf16[128,2,128]{0,2,1:T(8,128)(2,1)} %copy-done.5) | copy-start | bytes 196612
  370.2 28.1 %copy-start.3 = (bf16[128,512]{1,0:T(8,128)(2,1)S(1)}, bf16[128,512]{1,0:T(8,128)(2,1)}, u32[]{:S(2)}) copy-start(bf16[128,512]{1,0:T(8,128)(2,1)} %param.22) | copy-start | bytes 393220
  370.2 28.1 %copy-start.4 = (bf16[128,512]{1,0:T(8,128)(2,1)S(1)}, bf16[128,512]{1,0:T(8,128)(2,1)}, u32[]{:S(2)}) copy-start(bf16[128,512]{1,0:T(8,128)(2,1)} %reduce-scatter.3.cloned.1.call-done) | copy-start | bytes 393220
Sparse Core Ops, SparseCore 0:
  16.1 49.9 all-gather.4
  68.5 23.7 reduce-scatter.2
  94.6 109.6 all-gather.6
  206.4 102.8 all-gather.10
  311.4 58.7 all-gather.8
  378.4 19.8 reduce-scatter.4
